TPU v7x, 32 devices: a whole 2x2x4 slice. The times are simulated.
32 devices in a mesh: wide: 8 (over z, x), narrow: 4 (over y, core).
Axes of the slice: x: 2, y: 2, z: 4, core: 2. Of those that a mesh axis runs over, the one named last changes fastest.
Arguments:
- tile_data: bfloat16 [10240, 128, 128], P(('wide', 'narrow')), may hold values from -0.119628906 to 0.119628906
- tile_user: int32 [10240], P(('wide', 'narrow')), may hold values from 0 to 15
- tile_item: int32 [10240], P(('wide', 'narrow')), may hold values from 0 to 7
- tile_word: int32 [10240], P(('wide', 'narrow')), may hold values from 0 to 4095
- tile_month: int32 [10240], P(('wide', 'narrow')), may hold values from 0 to 999
- tile_live: int32 [32], P(('wide', 'narrow')), may hold values from 160 to 320, as said below
- user_need: int32 [32, 16], P(('wide', 'narrow')), may hold values from 0 to 127, as said below
- item_need: int32 [32, 8], P(('wide', 'narrow')), may hold values from 0 to 127, as said below
- user_slot: int32 [128], replicated, may hold values from 0 to 127, as said below
- item_slot: int32 [128], replicated, may hold values from 0 to 127, as said below
- user_factor: bfloat16 [16384, 128], P('wide'), may hold values from -6 to 6
- word_factor: bfloat16 [4096, 128], replicated, may hold values from -6 to 6
- month_factor: bfloat16 [1000, 128], replicated, may hold values from -6 to 6
Outputs:
- item_rows: float32 [16384, 128], P(('wide', 'narrow'))
Inputs may be any that keep to these rules, and one draw needn't show every extreme that they name: user_slot is a permutation; the owner of user block b is user_slot[b] // 16. item_slot is a permutation; the owner of item block b is item_slot[b] // 16. `user_need`: entries k * 2 to k * 2 + 1 of each row are distinct user blocks whose owner is k. `item_need`: entry k of each row is an item block whose owner is k. `tile_live`: some device has all its slots live.
All inputs are finite; a program needn't handle non-finite values.
Results may differ from a plain program's by a relative error of at most 0.0029.
Values may be sent and summed in bfloat16 or wider, within the bound.
No kernel may reach another device: no remote copies, remote signals or barrier semaphores. Data moves between devices by JAX's collectives and lax.ppermute only.
A program may use at most 128 MiB of HBM per device.

v0:
```python
import functools

import jax
import jax.numpy as jnp
from jax import lax
from jax.experimental import pallas as pl
from jax.experimental.pallas import tpu as pltpu
from jax.sharding import PartitionSpec as P

CONTRACT_MIB = 12
ANSWER_MIB = 12
RANK_MIB = 63
TURN_MIB = 12
TURN = 32
GROUP = 4
CHUNKS = 12
SMEM = pl.BlockSpec(memory_space=pltpu.SMEM)
VMEM = pl.BlockSpec(memory_space=pltpu.VMEM)
HBM = pl.BlockSpec(memory_space=pltpu.HBM)


def rank_kernel(
    slots, pad_count, me, live, user, item, plan, place_v, count_v, offset_v, place, count, offset, fetch
):
    tile_count = item.shape[0]
    touched = count.shape[1]
    dump = slots - 16
    rows = lax.broadcasted_iota(jnp.int32, (touched, tile_count), 0)
    lanes = lax.broadcasted_iota(jnp.int32, (touched, tile_count), 1)
    one = jnp.where((rows == item[...].reshape(1, tile_count)) & (lanes < live[0]), 1.0, 0.0)
    one_half = one.astype(jnp.bfloat16)
    before = jnp.where(
        lax.broadcasted_iota(jnp.int32, (tile_count, tile_count), 0)
        < lax.broadcasted_iota(jnp.int32, (tile_count, tile_count), 1),
        1.0,
        0.0,
    ).astype(jnp.bfloat16)
    rank = jnp.dot(one_half, before, preferred_element_type=jnp.float32)
    small_rows = lax.broadcasted_iota(jnp.int32, (touched, touched), 0)
    small_lanes = lax.broadcasted_iota(jnp.int32, (touched, touched), 1)
    chunks_of = lambda n: jnp.floor((n + (GROUP - 1)) * (1.0 / GROUP))
    count_column = jnp.sum(one, axis=1, keepdims=True)
    chunks_column = jnp.broadcast_to(chunks_of(count_column), (touched, 128)).astype(jnp.bfloat16)
    offset_column = GROUP * jnp.dot(
        jnp.where(small_lanes < small_rows, 1.0, 0.0).astype(jnp.bfloat16),
        chunks_column,
        preferred_element_type=jnp.float32,
    )[:, :1]
    here = jnp.sum(one * (rank + offset_column), axis=0, keepdims=True)
    lane = lax.broadcasted_iota(jnp.int32, (1, tile_count), 1)
    place_v[...] = jnp.where(lane < live[0], here.astype(jnp.int32), dump + lax.rem(lane, 16))
    count_row = lax.dot_general(
        jnp.ones((8, tile_count), jnp.bfloat16),
        one_half,
        (((1,), (1,)), ((), ())),
        preferred_element_type=jnp.float32,
    )
    offset_row = GROUP * jnp.dot(
        chunks_of(count_row).astype(jnp.bfloat16),
        jnp.where(small_rows < small_lanes, 1.0, 0.0).astype(jnp.bfloat16),
        preferred_element_type=jnp.float32,
    )
    count_v[...] = count_row.astype(jnp.int32)
    offset_v[...] = offset_row.astype(jnp.int32)
    fetched = [
        pltpu.make_async_copy(source, sink, fetch.at[n])
        for n, (source, sink) in enumerate(((place_v, place), (count_v, count), (offset_v, offset)))
    ]
    for copy in fetched:
        copy.start()
    for copy in fetched:
        copy.wait()
    places = slots + slots // GROUP + 1
    pads = places + tile_count
    for n in range(pad_count):
        plan[pads + n] = dump + n % 16
    plan[plan.shape[0] - 1] = me[0]

    def blank(n, p):
        plan[pads + n] = p
        plan[p] = 0

    def pad(q, blanks):
        first, n = offset[0, q], count[0, q]
        chunks = (n + GROUP - 1) // GROUP

        def mark(c, _):
            plan[slots + first // GROUP + c] = q
            return 0

        def fill(p, blanks):
            blank(blanks, p)
            return blanks + 1

        lax.fori_loop(0, chunks, mark, 0)
        return lax.fori_loop(first + n, first + chunks * GROUP, fill, blanks)

    blanks = lax.fori_loop(0, touched, pad, 0)
    last = offset[0, touched - 1] // GROUP
    chunks = last + (count[0, touched - 1] + GROUP - 1) // GROUP
    for c in range(CHUNKS - 1):
        plan[slots + chunks + c] = 0
        for g in range(GROUP):
            blank(blanks + c * GROUP + g, (chunks + c) * GROUP + g)
    plan[places - 1] = (chunks + CHUNKS - 1) // CHUNKS

    def put(c, _):
        for n in range(TURN):
            t = c * TURN + n
            p = place[0, t]
            plan[p] = user[t]
            plan[places + t] = p
        return 0

    lax.fori_loop(0, tile_count // TURN, put, 0)


def slots_for(tile_count, touched):
    per_step = GROUP * CHUNKS
    return -(-(tile_count + touched * (GROUP - 1)) // per_step) * per_step + per_step + 16


def rank(me, live, user, item, touched):
    tile_count = user.shape[0]
    slots = slots_for(tile_count, touched)
    pads = touched * (GROUP - 1) + (CHUNKS - 1) * GROUP
    return pl.pallas_call(
        functools.partial(rank_kernel, slots, pads),
        out_shape=jax.ShapeDtypeStruct(
            (slots + slots // GROUP + 1 + tile_count + pads + 1,), jnp.int32
        ),
        in_specs=[SMEM, SMEM, SMEM, VMEM],
        out_specs=SMEM,
        scratch_shapes=[
            pltpu.VMEM((1, tile_count), jnp.int32),
            pltpu.VMEM((8, touched), jnp.int32),
            pltpu.VMEM((8, touched), jnp.int32),
            pltpu.SMEM((1, tile_count), jnp.int32),
            pltpu.SMEM((8, touched), jnp.int32),
            pltpu.SMEM((8, touched), jnp.int32),
            pltpu.SemaphoreType.DMA((3,)),
        ],
        compiler_params=pltpu.CompilerParams(vmem_limit_bytes=RANK_MIB << 20),
        cost_estimate=pl.CostEstimate(flops=1 << 33, bytes_accessed=1 << 25, transcendentals=0),
        name="rank",
    )(me, live, user, item)


def turn_kernel(
    pad_count, plan, word, month, tiles, words, months, turned, scale, word_rows, month_rows
):
    tile_count = tiles.shape[0]
    slots = turned.shape[0]
    places = slots + slots // GROUP + 1
    word_rows[...] = words[...].astype(jnp.float32)
    month_rows[...] = months[...].astype(jnp.float32)
    nothing = jnp.zeros(turned.shape[1:], turned.dtype)
    no_scale = jnp.zeros((1, scale.shape[1]), scale.dtype)

    def clear(n, _):
        p = plan[places + tile_count + n]
        turned[p] = nothing
        scale[pl.ds(p, 1), :] = no_scale
        return 0

    lax.fori_loop(0, pad_count, clear, 0, unroll=4)

    def put(c, _):
        for n in range(TURN):
            t = c * TURN + n
            p = plan[places + t]
            turned[p] = tiles[t].T
            scale[pl.ds(p, 1), :] = (
                word_rows[pl.ds(word[t], 1), :] * month_rows[pl.ds(month[t], 1), :]
            )
        return 0

    lax.fori_loop(0, tile_count // TURN, put, 0)


def turn(plan, word, month, tiles, words, months, slots):
    tile_count, side = tiles.shape[:2]
    width = words.shape[1]
    pads = plan.shape[0] - (slots + slots // GROUP + 1 + tile_count) - 1
    return pl.pallas_call(
        functools.partial(turn_kernel, pads),
        out_shape=(
            jax.ShapeDtypeStruct((slots, side, side), tiles.dtype),
            jax.ShapeDtypeStruct((slots, width), jnp.float32),
        ),
        in_specs=[SMEM, SMEM, SMEM, VMEM, VMEM, VMEM],
        out_specs=(VMEM, VMEM),
        scratch_shapes=[
            pltpu.VMEM(words.shape, jnp.float32),
            pltpu.VMEM(months.shape, jnp.float32),
        ],
        compiler_params=pltpu.CompilerParams(vmem_limit_bytes=TURN_MIB << 20),
        cost_estimate=pl.CostEstimate(
            flops=1 << 30, bytes_accessed=4 * tiles.size, transcendentals=0
        ),
        name="turn",
    )(plan, word, month, tiles, words, months)


def ask_kernel(user_need, item_need, need):
    wide = need.shape[0]
    per_user, per_item = user_need.shape[1] // wide, item_need.shape[1] // wide
    for k in range(wide):
        for j in range(per_user):
            need[k, 0, j] = user_need[0, k * per_user + j]
        for j in range(per_item):
            need[k, 0, per_user + j] = item_need[0, k * per_item + j]


def ask(user_need, item_need, wide):
    per = (user_need.shape[1] + item_need.shape[1]) // wide
    return pl.pallas_call(
        ask_kernel,
        out_shape=jax.ShapeDtypeStruct((wide, 1, per), jnp.int32),
        in_specs=[SMEM, SMEM],
        out_specs=SMEM,
        compiler_params=pltpu.CompilerParams(vmem_limit_bytes=63 << 20),
        name="ask",
    )(user_need, item_need)


def answer_kernel(owned, per, me, heard, slot, blocks, *outs):
    for d, out in enumerate(outs):
        k = me[0] ^ d
        for j in range(per):
            out[j] = blocks[lax.rem(slot[heard[k, 0, j]], owned)]


def answer(me, heard, slot, blocks, per):
    owned, side, width = blocks.shape
    wide = heard.shape[0]
    return pl.pallas_call(
        functools.partial(answer_kernel, owned, per),
        out_shape=(jax.ShapeDtypeStruct((per, side, width), blocks.dtype),) * wide,
        in_specs=[SMEM, SMEM, SMEM, VMEM],
        out_specs=(VMEM,) * wide,
        compiler_params=pltpu.CompilerParams(vmem_limit_bytes=ANSWER_MIB << 20),
        cost_estimate=pl.CostEstimate(flops=1 << 33, bytes_accessed=1 << 25, transcendentals=0),
        name="answer",
    )(me, heard, slot, blocks)


def contract_kernel(plan, scale, turned, *refs):
    fetched, (out, wide_blocks, total) = refs[:-3], refs[-3:]
    per = fetched[0].shape[0]
    slots = scale.shape[0]
    per_step = GROUP * CHUNKS
    me = plan[plan.shape[0] - 1]
    for d, blocks in enumerate(fetched):
        for j in range(per):
            wide_blocks[(me ^ d) * per + j] = blocks[j].astype(jnp.float32)
    total[...] = jnp.zeros_like(total)

    def step(i, _):
        first = i * per_step
        for c in range(CHUNKS):
            left, right = [], []
            for g in range(GROUP):
                p = first + c * GROUP + g
                left.append(turned[p])
                right.append((wide_blocks[plan[p]] * scale[pl.ds(p, 1), :]).astype(jnp.bfloat16))
            part = jnp.dot(
                jnp.concatenate(left, 1),
                jnp.concatenate(right, 0),
                preferred_element_type=jnp.float32,
            )
            q = plan[slots + i * CHUNKS + c]
            total[q] = total[q] + part
        return 0

    lax.fori_loop(0, plan[slots + slots // GROUP], step, 0)
    out[...] = total[...].astype(out.dtype)


def contract(plan, scale, turned, fetched, touched):
    per, side, width = fetched[0].shape
    return pl.pallas_call(
        contract_kernel,
        out_shape=jax.ShapeDtypeStruct((touched, side, width), jnp.bfloat16),
        in_specs=[SMEM, VMEM, VMEM] + [VMEM] * len(fetched),
        out_specs=VMEM,
        scratch_shapes=[
            pltpu.VMEM((len(fetched) * per, side, width), jnp.float32),
            pltpu.VMEM((touched, side, width), jnp.float32),
        ],
        compiler_params=pltpu.CompilerParams(vmem_limit_bytes=CONTRACT_MIB << 20),
        cost_estimate=pl.CostEstimate(
            flops=2 * turned.size * width, bytes_accessed=turned.size, transcendentals=0
        ),
        name="contract",
    )(plan, scale, turned, *fetched)


def merge_kernel(items_owned, per, me, heard, slot, parts, mine, *rest):
    sends, total = rest[:-1], rest[-1]
    share = mine.shape[0]
    total[...] = jnp.zeros_like(total)

    base = heard.shape[2] - per

    def add(k, _):
        for n in range(per):
            j = lax.rem(slot[heard[k, 0, base + n]], items_owned)
            total[j] = total[j] + parts[k * per + n].astype(jnp.float32)
        return 0

    lax.fori_loop(0, heard.shape[0], add, 0)
    for d in range(items_owned // share):
        first = (me[0] ^ d) * share
        for j in range(share):
            if d == 0:
                mine[j] = total[first + j]
            else:
                sends[d - 1][j] = total[first + j].astype(jnp.bfloat16)


def merge(me, heard, slot, parts, items_owned, members, per):
    side, width = parts.shape[1:]
    share = items_owned // members
    piece = lambda kind: jax.ShapeDtypeStruct((share, side, width), kind)
    return pl.pallas_call(
        functools.partial(merge_kernel, items_owned, per),
        out_shape=(piece(jnp.float32),) + (piece(jnp.bfloat16),) * (members - 1),
        in_specs=[SMEM, SMEM, SMEM, VMEM],
        out_specs=(VMEM,) * members,
        scratch_shapes=[pltpu.VMEM((items_owned, side, width), jnp.float32)],
        compiler_params=pltpu.CompilerParams(vmem_limit_bytes=12 << 20),
        name="merge",
    )(me, heard, slot, parts)


def body(
    tile_data,
    tile_user,
    tile_item,
    tile_word,
    tile_month,
    tile_live,
    user_need,
    item_need,
    user_slot,
    item_slot,
    user_factor,
    word_factor,
    month_factor,
):
    wide = lax.axis_size("wide")
    members = lax.axis_size("narrow")
    side = tile_data.shape[1]
    width = user_factor.shape[1]
    touched = item_need.shape[1]
    items_owned = item_slot.shape[0] // wide
    per_user = user_need.shape[1] // wide
    heard = lax.all_to_all(
        ask(user_need, item_need, wide), "wide", split_axis=0, concat_axis=0, tiled=True
    )
    me_wide = lax.axis_index("wide").reshape(1)
    plan = rank(me_wide, tile_live, tile_user, tile_item, touched)
    replies = answer(me_wide, heard, user_slot, user_factor.reshape(-1, side, width), per_user)
    fetched = list(replies)
    for d in reversed(range(1, wide)):
        fetched[d] = lax.ppermute(replies[d], "wide", [(k, k ^ d) for k in range(wide)])
    turned, scale = turn(
        plan,
        tile_word,
        tile_month,
        tile_data,
        word_factor,
        month_factor,
        slots_for(tile_data.shape[0], touched),
    )
    partial = contract(plan, scale, turned, fetched, touched)
    arrived = lax.all_to_all(
        partial.reshape(wide, -1, side, width), "wide", split_axis=0, concat_axis=0, tiled=True
    ).reshape(-1, side, width)
    me = lax.axis_index("narrow").reshape(1)
    pieces = merge(me, heard, item_slot, arrived, items_owned, members, touched // wide)
    rows = pieces[0]
    for d in range(1, members):
        got = lax.ppermute(pieces[d], "narrow", [(n, n ^ d) for n in range(members)])
        rows = rows + got.astype(jnp.float32)
    return rows.reshape(-1, width)


def solution(mesh):
    return jax.shard_map(
        body,
        mesh=mesh,
        in_specs=(
            P(("wide", "narrow"), None, None),
            P(("wide", "narrow")),
            P(("wide", "narrow")),
            P(("wide", "narrow")),
            P(("wide", "narrow")),
            P(("wide", "narrow")),
            P(("wide", "narrow"), None),
            P(("wide", "narrow"), None),
            P(),
            P(),
            P("wide", None),
            P(),
            P(),
        ),
        out_specs=P(("wide", "narrow"), None),
        check_vma=False,
    )
```

profile of v0, /device:TPU:0, one launch (start us, length us, event | category | flops | bytes accessed | tf_op | source)
XLA Modules:
  0.0 70.0 jit_solution(12505479586135569507)
XLA Ops:
  0.0 1.3 %ask.1 = s32[8,1,3]{2,1,0:T(1,128)} custom-call(s32[1,16]{1,0:T(1,128)} %user_need.1, s32[1,8]{1,0:T(1,128)} %item_need.1), custom_call_target="tpu_custom_call" | custom-call | tf_op jit(solution)/shard_map/ask/pallas_call | solution.py:217
  1.3 7.3 %all-to-all-start = ((s32[8,1,3]{2,1,0:T(1,128)}), s32[8,1,3]{2,1,0:T(1,128)S(1)}, u32[]{:S(2)}, u32[]{:S(2)}) async-start(s32[8,1,3]{2,1,0:T(1,128)} %ask.1), calls=%async_computation | async-start | bytes 8192 | tf_op jit(solution)/shard_map/all_to_all | solution.py:359
  9.2 5.8 %all-to-all-done.heard = s32[8,1,3]{2,1,0:T(1,128)S(1)} async-done(((s32[8,1,3]{2,1,0:T(1,128)}), s32[8,1,3]{2,1,0:T(1,128)S(1)}, u32[]{:S(2)}, u32[]{:S(2)}) %all-to-all-start) | async-done | bytes 128 | tf_op jit(solution)/shard_map/all_to_all | solution.py:359
  15.0 0.0 copy-start.7
  15.0 1.0 %copy-done.7 = bf16[2048,128]{1,0:T(8,128)(2,1)S(1)} copy-done((bf16[2048,128]{1,0:T(8,128)(2,1)S(1)}, bf16[2048,128]{1,0:T(8,128)(2,1)}, u32[]{:S(2)}) %copy-start.7) | copy-done | bytes 524312
  16.0 0.0 copy-start.8
  16.1 0.7 copy-done.8
  16.7 0.7 answer.1
  17.4 0.6 collective-permute-start
  18.0 0.0 copy-start.2
  18.0 0.0 copy-start.4
  18.0 0.0 copy-start.5
  18.0 0.6 collective-permute-start.1
  18.6 4.2 %rank.1.plan = s32[950]{0:T(1024)} custom-call(s32[1]{0:T(128)} %bitcast.1.me, s32[1]{0:T(128)S(6)} %copy.15.live, s32[320]{0:T(512)} %user.1, s32[320]{0:T(512)} %item.1), custom_call_target="tpu_custom_call" | custom-call | flops 8589934592 | bytes 33554432 | tf_op jit(solution)/shard_map/rank/pallas_call | solution.py:127
  22.7 0.0 copy-start.6
  22.8 2.2 %collective-permute-start.2 = (bf16[2,128,128]{2,1,0:T(8,128)(2,1)S(1)}, bf16[2,128,128]{2,1,0:T(8,128)(2,1)S(1)}, u32[]{:S(2)}, u32[]{:S(2)}) collective-permute-start(bf16[2,128,128]{2,1,0:T(8,128)(2,1)S(1)} %get-tuple-element.24), channel_id=1, source_target_pairs={{0,12},{4,8},{8,4},{12,0},{16,28},{20,24},{24,20},{28,16},{1,13},{... | collective-permute-start | bytes 196616 | tf_op jit(solution)/shard_map/ppermute | solution.py:367
  24.9 0.5 collective-permute-start.3
  25.4 2.7 %collective-permute-start.4 = (bf16[2,128,128]{2,1,0:T(8,128)(2,1)S(1)}, bf16[2,128,128]{2,1,0:T(8,128)(2,1)S(1)}, u32[]{:S(2)}, u32[]{:S(2)}) collective-permute-start(bf16[2,128,128]{2,1,0:T(8,128)(2,1)S(1)} %get-tuple-element.26), channel_id=1, source_target_pairs={{0,20},{4,16},{8,28},{12,24},{16,4},{20,0},{24,12},{28,8},{1,21},{... | collective-permute-start | bytes 196616 | tf_op jit(solution)/shard_map/ppermute | solution.py:367
  28.1 0.0 collective-permute-done.refs_1_
  28.1 0.3 collective-permute-start.5
  28.4 0.0 collective-permute-done.1.refs_2_
  28.4 4.2 %collective-permute-start.6 = (bf16[2,128,128]{2,1,0:T(8,128)(2,1)S(1)}, bf16[2,128,128]{2,1,0:T(8,128)(2,1)S(1)}, u32[]{:S(2)}, u32[]{:S(2)}) collective-permute-start(bf16[2,128,128]{2,1,0:T(8,128)(2,1)S(1)} %get-tuple-element.28), channel_id=1, source_target_pairs={{0,28},{4,24},{8,20},{12,16},{16,12},{20,8},{24,4},{28,0},{1,29},{... | collective-permute-start | bytes 196616 | tf_op jit(solution)/shard_map/ppermute | solution.py:367
  32.6 0.0 copy-done.2
  32.6 0.0 copy-done.4
  32.6 0.0 copy-done.5
  32.6 0.0 copy-start
  32.6 4.0 %copy-done = bf16[320,128,128]{2,1,0:T(8,128)(2,1)S(1)} copy-done((bf16[320,128,128]{2,1,0:T(8,128)(2,1)S(1)}, bf16[320,128,128]{2,1,0:T(8,128)(2,1)}, u32[]{:S(2)}) %copy-start) | copy-done | bytes 10485784
  36.6 0.0 copy-start.1
  36.6 1.2 %copy-done.1 = bf16[4096,128]{1,0:T(8,128)(2,1)S(1)} copy-done((bf16[4096,128]{1,0:T(8,128)(2,1)S(1)}, bf16[4096,128]{1,0:T(8,128)(2,1)}, u32[]{:S(2)}) %copy-start.1) | copy-done | bytes 1048600
  37.8 0.7 copy-done.3
  38.5 4.5 %turn.1 = (bf16[448,128,128]{2,1,0:T(8,128)(2,1)S(1)}, f32[448,128]{1,0:T(8,128)S(1)}) custom-call(s32[950]{0:T(1024)S(1)} %copy-done.3, s32[320]{0:T(512)S(1)} %copy-done.4, s32[320]{0:T(512)S(1)} %copy-done.5, bf16[320,128,128]{2,1,0:T(8,128)(2,1)S(1)} %copy-done, bf16[4096,128]{1,0:T(8,128)(2,1)S(1)} %copy-done.1, bf16[1000,128]{1,0:T(8,128)(2,1)S(1)} %copy-done.2), custom_call_target="tpu_custom_call" | custom-call | flops 1073741824 | bytes 20971520 | tf_op jit(solution)/shard_map/turn/pallas_call | solution.py:185
  43.0 0.0 collective-permute-done.2.refs_3_
  43.0 0.0 collective-permute-done.3.refs_4_
  43.0 0.0 collective-permute-done.4.refs_5_
  43.0 0.0 collective-permute-done.5.refs_6_
  43.1 0.0 collective-permute-done.6.refs_7_
  43.1 5.4 %contract.1 = bf16[8,128,128]{2,1,0:T(8,128)(2,1)} custom-call(s32[950]{0:T(1024)S(1)} %copy-done.3, f32[448,128]{1,0:T(8,128)S(1)} %get-tuple-element.19.scale, bf16[448,128,128]{2,1,0:T(8,128)(2,1)S(1)} %get-tuple-element.20.turned, bf16[2,128,128]{2,1,0:T(8,128)(2,1)S(1)} %get-tuple-element.21.refs_0_, ...), custom_call_target="tpu_custom_call" | custom-call | flops 1879048192 | bytes 7340032 | tf_op jit(solution)/shard_map/contract/pallas_call | solution.py:282
  48.5 3.4 %all-to-all-start.1 = ((bf16[8,1,128,128]{3,2,1,0:T(8,128)(2,1)}), bf16[8,1,128,128]{3,2,1,0:T(8,128)(2,1)S(1)}, u32[]{:S(2)}, u32[]{:S(2)}) async-start(bf16[8,1,128,128]{3,2,1,0:T(8,128)(2,1)} %bitcast.4), calls=%async_computation.1 | async-start | bytes 524288 | tf_op jit(solution)/shard_map/all_to_all | solution.py:378
  51.9 8.2 %all-to-all-done.1 = bf16[8,1,128,128]{3,2,1,0:T(8,128)(2,1)S(1)} async-done(((bf16[8,1,128,128]{3,2,1,0:T(8,128)(2,1)}), bf16[8,1,128,128]{3,2,1,0:T(8,128)(2,1)S(1)}, u32[]{:S(2)}, u32[]{:S(2)}) %all-to-all-start.1) | async-done | bytes 262176 | tf_op jit(solution)/shard_map/all_to_all | solution.py:378
  60.1 0.0 copy-done.6
  60.1 0.9 %merge.1 = (f32[4,128,128]{2,1,0:T(8,128)S(1)}, bf16[4,128,128]{2,1,0:T(8,128)(2,1)S(1)}, bf16[4,128,128]{2,1,0:T(8,128)(2,1)S(1)}, bf16[4,128,128]{2,1,0:T(8,128)(2,1)S(1)}) custom-call(s32[1]{0:T(128)} %bitcast.me, s32[8,1,3]{2,1,0:T(1,128)S(1)} %all-to-all-done.heard, s32[128]{0:T(128)S(1)} %copy-done.6, bf16[8,128,128]{2,1,0:T(8,128)(2,1)S(1)} %bitcast.8), custom_call_target="tpu_custom_call" | custom-call | tf_op jit(solution)/shard_map/merge/pallas_call | solution.py:326
  61.0 0.1 collective-permute-start.7
  61.0 0.5 collective-permute-start.8
  61.5 1.4 %collective-permute-start.9 = (bf16[4,128,128]{2,1,0:T(8,128)(2,1)S(1)}, bf16[4,128,128]{2,1,0:T(8,128)(2,1)S(1)}, u32[]{:S(2)}, u32[]{:S(2)}) collective-permute-start(bf16[4,128,128]{2,1,0:T(8,128)(2,1)S(1)} %get-tuple-element.32), channel_id=1, source_target_pairs={{0,3},{1,2},{2,1},{3,0},{4,7},{5,6},{6,5},{7,4},{8,11},{9,10},{10,... | collective-permute-start | bytes 393224 | tf_op jit(solution)/shard_map/ppermute | solution.py:385
  62.9 0.0 collective-permute-done.7
  62.9 4.6 %collective-permute-done.8 = bf16[4,128,128]{2,1,0:T(8,128)(2,1)S(1)} collective-permute-done((bf16[4,128,128]{2,1,0:T(8,128)(2,1)S(1)}, bf16[4,128,128]{2,1,0:T(8,128)(2,1)S(1)}, u32[]{:S(2)}, u32[]{:S(2)}) %collective-permute-start.8) | collective-permute-done | bytes 131104 | tf_op jit(solution)/shard_map/ppermute | solution.py:385
  67.5 1.7 %collective-permute-done.9 = bf16[4,128,128]{2,1,0:T(8,128)(2,1)S(1)} collective-permute-done((bf16[4,128,128]{2,1,0:T(8,128)(2,1)S(1)}, bf16[4,128,128]{2,1,0:T(8,128)(2,1)S(1)}, u32[]{:S(2)}, u32[]{:S(2)}) %collective-permute-start.9) | collective-permute-done | bytes 131104 | tf_op jit(solution)/shard_map/ppermute | solution.py:385
  69.2 0.8 %convert_add_fusion = f32[4,128,128]{2,1,0:T(8,128)} fusion(bf16[4,128,128]{2,1,0:T(8,128)(2,1)S(1)} %collective-permute-done.9, bf16[4,128,128]{2,1,0:T(8,128)(2,1)S(1)} %collective-permute-done.8, f32[4,128,128]{2,1,0:T(8,128)S(1)} %get-tuple-element.29, bf16[4,128,128]{2,1,0:T(8,128)(2,1)S(1)} %collective-permute-done.7), kind=kLoop, calls=%fused_computation | loop fusion | flops 393216 | bytes 917504 | tf_op jit(solution)/shard_map/add | solution.py:386
  (1 shorter events, 0.0 us)
Async XLA Ops:
  1.3 13.7 %all-to-all-start = ((s32[8,1,3]{2,1,0:T(1,128)}), s32[8,1,3]{2,1,0:T(1,128)S(1)}, u32[]{:S(2)}, u32[]{:S(2)}) async-start(s32[8,1,3]{2,1,0:T(1,128)} %ask.1), calls=%async_computation | async-start | bytes 8192 | tf_op jit(solution)/shard_map/all_to_all | solution.py:359
  15.0 1.0 %copy-start.7 = (bf16[2048,128]{1,0:T(8,128)(2,1)S(1)}, bf16[2048,128]{1,0:T(8,128)(2,1)}, u32[]{:S(2)}) copy-start(bf16[2048,128]{1,0:T(8,128)(2,1)} %param.23) | copy-start | bytes 1572868
  16.0 0.7 copy-start.8
  17.4 10.8 %collective-permute-start = (bf16[2,128,128]{2,1,0:T(8,128)(2,1)S(1)}, bf16[2,128,128]{2,1,0:T(8,128)(2,1)S(1)}, u32[]{:S(2)}, u32[]{:S(2)}) collective-permute-start(bf16[2,128,128]{2,1,0:T(8,128)(2,1)S(1)} %get-tuple-element.22), channel_id=1, source_target_pairs={{0,4},{4,0},{8,12},{12,8},{16,20},{20,16},{24,28},{28,24},{1,5},{5... | collective-permute-start | bytes 196616 | tf_op jit(solution)/shard_map/ppermute | solution.py:367
  18.0 14.6 %copy-start.2 = (bf16[1000,128]{1,0:T(8,128)(2,1)S(1)}, bf16[1000,128]{1,0:T(8,128)(2,1)}, u32[]{:S(2)}) copy-start(bf16[1000,128]{1,0:T(8,128)(2,1)} %months.1) | copy-start | bytes 768004
  18.0 14.6 %copy-start.4 = (s32[320]{0:T(512)S(1)}, s32[320]{0:T(512)}, u32[]{:S(2)}) copy-start(s32[320]{0:T(512)} %word.1) | copy-start | bytes 3844
  18.0 14.6 %copy-start.5 = (s32[320]{0:T(512)S(1)}, s32[320]{0:T(512)}, u32[]{:S(2)}) copy-start(s32[320]{0:T(512)} %month.1) | copy-start | bytes 3844
  18.0 10.4 %collective-permute-start.1 = (bf16[2,128,128]{2,1,0:T(8,128)(2,1)S(1)}, bf16[2,128,128]{2,1,0:T(8,128)(2,1)S(1)}, u32[]{:S(2)}, u32[]{:S(2)}) collective-permute-start(bf16[2,128,128]{2,1,0:T(8,128)(2,1)S(1)} %get-tuple-element.23), channel_id=1, source_target_pairs={{0,8},{4,12},{8,0},{12,4},{16,24},{20,28},{24,16},{28,20},{1,9},{5... | collective-permute-start | bytes 196616 | tf_op jit(solution)/shard_map/ppermute | solution.py:367
  22.7 37.4 %copy-start.6 = (s32[128]{0:T(128)S(1)}, s32[128]{0:T(128)}, u32[]{:S(2)}) copy-start(s32[128]{0:T(128)} %slot.3) | copy-start | bytes 1540
  22.8 20.3 %collective-permute-start.2 = (bf16[2,128,128]{2,1,0:T(8,128)(2,1)S(1)}, bf16[2,128,128]{2,1,0:T(8,128)(2,1)S(1)}, u32[]{:S(2)}, u32[]{:S(2)}) collective-permute-start(bf16[2,128,128]{2,1,0:T(8,128)(2,1)S(1)} %get-tuple-element.24), channel_id=1, source_target_pairs={{0,12},{4,8},{8,4},{12,0},{16,28},{20,24},{24,20},{28,16},{1,13},{... | collective-permute-start | bytes 196616 | tf_op jit(solution)/shard_map/ppermute | solution.py:367
  24.9 18.1 %collective-permute-start.3 = (bf16[2,128,128]{2,1,0:T(8,128)(2,1)S(1)}, bf16[2,128,128]{2,1,0:T(8,128)(2,1)S(1)}, u32[]{:S(2)}, u32[]{:S(2)}) collective-permute-start(bf16[2,128,128]{2,1,0:T(8,128)(2,1)S(1)} %get-tuple-element.25), channel_id=1, source_target_pairs={{0,16},{4,20},{8,24},{12,28},{16,0},{20,4},{24,8},{28,12},{1,17},{... | collective-permute-start | bytes 196616 | tf_op jit(solution)/shard_map/ppermute | solution.py:367
  25.4 17.6 %collective-permute-start.4 = (bf16[2,128,128]{2,1,0:T(8,128)(2,1)S(1)}, bf16[2,128,128]{2,1,0:T(8,128)(2,1)S(1)}, u32[]{:S(2)}, u32[]{:S(2)}) collective-permute-start(bf16[2,128,128]{2,1,0:T(8,128)(2,1)S(1)} %get-tuple-element.26), channel_id=1, source_target_pairs={{0,20},{4,16},{8,28},{12,24},{16,4},{20,0},{24,12},{28,8},{1,21},{... | collective-permute-start | bytes 196616 | tf_op jit(solution)/shard_map/ppermute | solution.py:367
  28.1 14.9 %collective-permute-start.5 = (bf16[2,128,128]{2,1,0:T(8,128)(2,1)S(1)}, bf16[2,128,128]{2,1,0:T(8,128)(2,1)S(1)}, u32[]{:S(2)}, u32[]{:S(2)}) collective-permute-start(bf16[2,128,128]{2,1,0:T(8,128)(2,1)S(1)} %get-tuple-element.27), channel_id=1, source_target_pairs={{0,24},{4,28},{8,16},{12,20},{16,8},{20,12},{24,0},{28,4},{1,25},{... | collective-permute-start | bytes 196616 | tf_op jit(solution)/shard_map/ppermute | solution.py:367
  28.4 14.6 %collective-permute-start.6 = (bf16[2,128,128]{2,1,0:T(8,128)(2,1)S(1)}, bf16[2,128,128]{2,1,0:T(8,128)(2,1)S(1)}, u32[]{:S(2)}, u32[]{:S(2)}) collective-permute-start(bf16[2,128,128]{2,1,0:T(8,128)(2,1)S(1)} %get-tuple-element.28), channel_id=1, source_target_pairs={{0,28},{4,24},{8,20},{12,16},{16,12},{20,8},{24,4},{28,0},{1,29},{... | collective-permute-start | bytes 196616 | tf_op jit(solution)/shard_map/ppermute | solution.py:367
  32.6 4.0 %copy-start = (bf16[320,128,128]{2,1,0:T(8,128)(2,1)S(1)}, bf16[320,128,128]{2,1,0:T(8,128)(2,1)}, u32[]{:S(2)}) copy-start(bf16[320,128,128]{2,1,0:T(8,128)(2,1)} %tiles.1) | copy-start | bytes 31457284
  36.6 1.2 %copy-start.1 = (bf16[4096,128]{1,0:T(8,128)(2,1)S(1)}, bf16[4096,128]{1,0:T(8,128)(2,1)}, u32[]{:S(2)}) copy-start(bf16[4096,128]{1,0:T(8,128)(2,1)} %words.1) | copy-start | bytes 3145732
  37.8 0.7 copy-start.3
  48.5 11.6 %all-to-all-start.1 = ((bf16[8,1,128,128]{3,2,1,0:T(8,128)(2,1)}), bf16[8,1,128,128]{3,2,1,0:T(8,128)(2,1)S(1)}, u32[]{:S(2)}, u32[]{:S(2)}) async-start(bf16[8,1,128,128]{3,2,1,0:T(8,128)(2,1)} %bitcast.4), calls=%async_computation.1 | async-start | bytes 524288 | tf_op jit(solution)/shard_map/all_to_all | solution.py:378
  61.0 1.9 %collective-permute-start.7 = (bf16[4,128,128]{2,1,0:T(8,128)(2,1)S(1)}, bf16[4,128,128]{2,1,0:T(8,128)(2,1)S(1)}, u32[]{:S(2)}, u32[]{:S(2)}) collective-permute-start(bf16[4,128,128]{2,1,0:T(8,128)(2,1)S(1)} %get-tuple-element.30), channel_id=1, source_target_pairs={{0,1},{1,0},{2,3},{3,2},{4,5},{5,4},{6,7},{7,6},{8,9},{9,8},{10,11... | collective-permute-start | bytes 393224 | tf_op jit(solution)/shard_map/ppermute | solution.py:385
  61.0 6.4 %collective-permute-start.8 = (bf16[4,128,128]{2,1,0:T(8,128)(2,1)S(1)}, bf16[4,128,128]{2,1,0:T(8,128)(2,1)S(1)}, u32[]{:S(2)}, u32[]{:S(2)}) collective-permute-start(bf16[4,128,128]{2,1,0:T(8,128)(2,1)S(1)} %get-tuple-element.31), channel_id=1, source_target_pairs={{0,2},{1,3},{2,0},{3,1},{4,6},{5,7},{6,4},{7,5},{8,10},{9,11},{10,... | collective-permute-start | bytes 393224 | tf_op jit(solution)/shard_map/ppermute | solution.py:385
  61.5 7.7 %collective-permute-start.9 = (bf16[4,128,128]{2,1,0:T(8,128)(2,1)S(1)}, bf16[4,128,128]{2,1,0:T(8,128)(2,1)S(1)}, u32[]{:S(2)}, u32[]{:S(2)}) collective-permute-start(bf16[4,128,128]{2,1,0:T(8,128)(2,1)S(1)} %get-tuple-element.32), channel_id=1, source_target_pairs={{0,3},{1,2},{2,1},{3,0},{4,7},{5,6},{6,5},{7,4},{8,11},{9,10},{10,... | collective-permute-start | bytes 393224 | tf_op jit(solution)/shard_map/ppermute | solution.py:385
where the time goes:
time: 70.4 us; the launch traced here: 70 us
  starting transfers between devices  23.6 us (34%)
  waiting for transfers between devices  20.3 us (29%)
  Pallas kernels  16.9 us (24%)
  local copies, waits for them, and re-layouts  7.6 us (11%)
  between operations  0.78 us (1%)
  other arithmetic  0.76 us (1%)
    ppermute x7, starting transfers between devices, body(): lax.ppermute(replies[d], 'wide', [(k, k ^ d) for k in range(wide)])  11 us
    all_to_all x1, waiting for transfers between devices, body(): lax.all_to_all(partial.reshape(wide, -1, side, width), 'wide', split_axis...  8.15 us
    unnamed x18, local copies, waits for them, and re-layouts  7.6 us
    all_to_all x1, starting transfers between devices, body(): lax.all_to_all(ask(user_need, item_need, wide), 'wide', split_axis=0, con...  7.29 us
    ppermute x3, waiting for transfers between devices, body(): lax.ppermute(pieces[d], 'narrow', [(n, n ^ d) for n in range(members)])  6.32 us
    all_to_all x1, waiting for transfers between devices, body(): lax.all_to_all(ask(user_need, item_need, wide), 'wide', split_axis=0, con...  5.77 us
    pallas_call x1, Pallas kernels, contract(): pl.pallas_call(contract_kernel, out_shape=jax.ShapeDtypeStruct((touched,...  5.45 us
    pallas_call x1, Pallas kernels, turn(): pl.pallas_call(functools.partial(turn_kernel, pads), out_shape=(jax.Shape...  4.52 us
  transfers between devices with their start and end apart: 12, of which 4 were waited for; matrix products, arithmetic and copies ran while one was open for 0% of the time, Pallas kernels for 12%

commit v1 on v0

v1 whole, which is shorter than its diff:
```python
import functools

import jax
import jax.numpy as jnp
from jax import lax
from jax.experimental import pallas as pl
from jax.experimental.pallas import tpu as pltpu
from jax.sharding import PartitionSpec as P

CONTRACT_MIB = 12
ANSWER_MIB = 12
RANK_MIB = 63
TURN_MIB = 12
TURN = 32
PADS = 8
GROUP = 4
CHUNKS = 12
SMEM = pl.BlockSpec(memory_space=pltpu.SMEM)
VMEM = pl.BlockSpec(memory_space=pltpu.VMEM)
HBM = pl.BlockSpec(memory_space=pltpu.HBM)


def rank_kernel(slots, touched, me, live, user, item, plan):
    tile_count = item.shape[0]
    dump = slots - 16
    iota = lambda shape, dim: lax.broadcasted_iota(jnp.int32, shape, dim)
    as_half = lambda mask: jnp.where(mask, 1.0, 0.0).astype(jnp.bfloat16)
    lane = iota((1, tile_count), 1)
    alive = lane < live[...].reshape(1, 1)
    one = jnp.where((iota((touched, tile_count), 0) == item[...].reshape(1, tile_count)) & alive, 1.0, 0.0)
    before = as_half(iota((tile_count, tile_count), 0) < iota((tile_count, tile_count), 1))
    earlier = jnp.dot(one.astype(jnp.bfloat16), before, preferred_element_type=jnp.float32)
    count = jnp.sum(one, axis=1, keepdims=True)
    chunks = jnp.floor((count + (GROUP - 1)) * (1.0 / GROUP))
    offset = GROUP * jnp.dot(
        as_half(iota((touched, touched), 1) < iota((touched, touched), 0)),
        jnp.broadcast_to(chunks, (touched, 128)).astype(jnp.bfloat16),
        preferred_element_type=jnp.float32,
    )[:, :1]
    here = jnp.sum(one * (earlier + offset), axis=0, keepdims=True).astype(jnp.int32)
    place = jnp.where(alive, here, dump + lax.rem(lane, 16))
    users = lax.dot_general(
        jnp.broadcast_to(user[...].reshape(1, tile_count), (8, tile_count)).astype(jnp.float32).astype(jnp.bfloat16),
        as_half(iota((slots, tile_count), 0) == place),
        (((1,), (1,)), ((), ())),
        preferred_element_type=jnp.float32,
    )
    offset, count = offset.astype(jnp.int32), count.astype(jnp.int32)
    size = GROUP * chunks.astype(jnp.int32)
    used = jnp.sum(size, axis=0, keepdims=True)
    width = plan.shape[1]
    passed = jnp.where(GROUP * iota((touched, width), 1) >= offset + size, 1, 0)
    plan[0:1, 0:slots] = users[0:1].astype(jnp.int32)
    plan[1:2, :] = jnp.minimum(jnp.sum(passed, axis=0, keepdims=True), touched - 1)
    plan[2:3, 0:tile_count] = place
    plan[3:4, :] = used + iota((1, width), 1)
    plan[4:5, :] = jnp.broadcast_to(used, (1, width))
    plan[5:6, :] = jnp.broadcast_to(me[0], (1, width))
    column = iota((touched, 128), 1)
    plan[PADS : PADS + touched, 0:128] = jnp.where(
        column < size - count, offset + count + column, dump + lax.rem(column, 16)
    )


def slots_for(tile_count, touched):
    per_step = GROUP * CHUNKS
    return -(-(tile_count + touched * (GROUP - 1)) // per_step) * per_step + per_step + 16


def rank(me, live, user, item, touched):
    slots = slots_for(user.shape[0], touched)
    return pl.pallas_call(
        functools.partial(rank_kernel, slots, touched),
        out_shape=jax.ShapeDtypeStruct((PADS + touched, -(-slots // 128) * 128), jnp.int32),
        in_specs=[SMEM, VMEM, VMEM, VMEM],
        out_specs=VMEM,
        compiler_params=pltpu.CompilerParams(vmem_limit_bytes=RANK_MIB << 20),
        cost_estimate=pl.CostEstimate(flops=1 << 33, bytes_accessed=1 << 25, transcendentals=0),
        name="rank",
    )(me, live, user, item)


def turn_kernel(plan, word, month, tiles, words, months, turned, scale, word_rows, month_rows):
    tile_count = tiles.shape[0]
    word_rows[...] = words[...].astype(jnp.float32)
    month_rows[...] = months[...].astype(jnp.float32)
    nothing = jnp.zeros(turned.shape[1:], turned.dtype)
    no_scale = jnp.zeros((1, scale.shape[1]), scale.dtype)

    def clear(p):
        turned[p] = nothing
        scale[pl.ds(p, 1), :] = no_scale

    def clear_item(q, _):
        for j in range(GROUP - 1):
            clear(plan[PADS + q, j])
        return 0

    lax.fori_loop(0, plan.shape[0] - PADS, clear_item, 0)

    def clear_rest(n, _):
        clear(plan[3, n])
        return 0

    lax.fori_loop(0, GROUP * (CHUNKS - 1), clear_rest, 0, unroll=4)

    def put(c, _):
        for n in range(TURN):
            t = c * TURN + n
            p = plan[2, t]
            turned[p] = tiles[t].T
            scale[pl.ds(p, 1), :] = (
                word_rows[pl.ds(word[t], 1), :] * month_rows[pl.ds(month[t], 1), :]
            )
        return 0

    lax.fori_loop(0, tile_count // TURN, put, 0)


def turn(plan, word, month, tiles, words, months, slots):
    side = tiles.shape[1]
    width = words.shape[1]
    return pl.pallas_call(
        turn_kernel,
        out_shape=(
            jax.ShapeDtypeStruct((slots, side, side), tiles.dtype),
            jax.ShapeDtypeStruct((slots, width), jnp.float32),
        ),
        in_specs=[SMEM, SMEM, SMEM, VMEM, VMEM, VMEM],
        out_specs=(VMEM, VMEM),
        scratch_shapes=[
            pltpu.VMEM(words.shape, jnp.float32),
            pltpu.VMEM(months.shape, jnp.float32),
        ],
        compiler_params=pltpu.CompilerParams(vmem_limit_bytes=TURN_MIB << 20),
        cost_estimate=pl.CostEstimate(
            flops=1 << 30, bytes_accessed=4 * tiles.size, transcendentals=0
        ),
        name="turn",
    )(plan, word, month, tiles, words, months)


def answer_kernel(owned, per, me, heard, slot, blocks, *outs):
    for d, out in enumerate(outs):
        k = me[0] ^ d
        for j in range(per):
            out[j] = blocks[lax.rem(slot[heard[k, 0, me[0] * per + j]], owned)]


def answer(me, heard, slot, blocks, per):
    owned, side, width = blocks.shape
    wide = heard.shape[0]
    return pl.pallas_call(
        functools.partial(answer_kernel, owned, per),
        out_shape=(jax.ShapeDtypeStruct((per, side, width), blocks.dtype),) * wide,
        in_specs=[SMEM, SMEM, SMEM, VMEM],
        out_specs=(VMEM,) * wide,
        compiler_params=pltpu.CompilerParams(vmem_limit_bytes=ANSWER_MIB << 20),
        cost_estimate=pl.CostEstimate(flops=1 << 33, bytes_accessed=1 << 25, transcendentals=0),
        name="answer",
    )(me, heard, slot, blocks)


def contract_kernel(plan, scale, turned, *refs):
    fetched, (out, wide_blocks, total) = refs[:-3], refs[-3:]
    per = fetched[0].shape[0]
    per_step = GROUP * CHUNKS
    me = plan[5, 0]
    for d, blocks in enumerate(fetched):
        for j in range(per):
            wide_blocks[(me ^ d) * per + j] = blocks[j].astype(jnp.float32)
    total[...] = jnp.zeros_like(total)

    def step(i, _):
        first = i * per_step
        for c in range(CHUNKS):
            left, right = [], []
            for g in range(GROUP):
                p = first + c * GROUP + g
                left.append(turned[p])
                right.append((wide_blocks[plan[0, p]] * scale[pl.ds(p, 1), :]).astype(jnp.bfloat16))
            part = jnp.dot(
                jnp.concatenate(left, 1),
                jnp.concatenate(right, 0),
                preferred_element_type=jnp.float32,
            )
            q = plan[1, i * CHUNKS + c]
            total[q] = total[q] + part
        return 0

    steps = (plan[4, 0] + per_step - 1) // per_step
    lax.fori_loop(0, steps, step, 0)
    out[...] = total[...].astype(out.dtype)


def contract(plan, scale, turned, fetched, touched):
    per, side, width = fetched[0].shape
    return pl.pallas_call(
        contract_kernel,
        out_shape=jax.ShapeDtypeStruct((touched, side, width), jnp.bfloat16),
        in_specs=[SMEM, VMEM, VMEM] + [VMEM] * len(fetched),
        out_specs=VMEM,
        scratch_shapes=[
            pltpu.VMEM((len(fetched) * per, side, width), jnp.float32),
            pltpu.VMEM((touched, side, width), jnp.float32),
        ],
        compiler_params=pltpu.CompilerParams(vmem_limit_bytes=CONTRACT_MIB << 20),
        cost_estimate=pl.CostEstimate(
            flops=2 * turned.size * width, bytes_accessed=turned.size, transcendentals=0
        ),
        name="contract",
    )(plan, scale, turned, *fetched)


def merge_kernel(items_owned, per, owner, me, heard, slot, parts, mine, *rest):
    sends, total = rest[:-1], rest[-1]
    share = mine.shape[0]
    total[...] = jnp.zeros_like(total)

    base = heard.shape[2] - per * heard.shape[0] + per * owner[0]

    def add(k, _):
        for n in range(per):
            j = lax.rem(slot[heard[k, 0, base + n]], items_owned)
            total[j] = total[j] + parts[k * per + n].astype(jnp.float32)
        return 0

    lax.fori_loop(0, heard.shape[0], add, 0)
    for d in range(items_owned // share):
        first = (me[0] ^ d) * share
        for j in range(share):
            if d == 0:
                mine[j] = total[first + j]
            else:
                sends[d - 1][j] = total[first + j].astype(jnp.bfloat16)


def merge(owner, me, heard, slot, parts, items_owned, members, per):
    side, width = parts.shape[1:]
    share = items_owned // members
    piece = lambda kind: jax.ShapeDtypeStruct((share, side, width), kind)
    return pl.pallas_call(
        functools.partial(merge_kernel, items_owned, per),
        out_shape=(piece(jnp.float32),) + (piece(jnp.bfloat16),) * (members - 1),
        in_specs=[SMEM, SMEM, SMEM, SMEM, VMEM],
        out_specs=(VMEM,) * members,
        scratch_shapes=[pltpu.VMEM((items_owned, side, width), jnp.float32)],
        compiler_params=pltpu.CompilerParams(vmem_limit_bytes=12 << 20),
        name="merge",
    )(owner, me, heard, slot, parts)


def body(
    tile_data,
    tile_user,
    tile_item,
    tile_word,
    tile_month,
    tile_live,
    user_need,
    item_need,
    user_slot,
    item_slot,
    user_factor,
    word_factor,
    month_factor,
):
    wide = lax.axis_size("wide")
    members = lax.axis_size("narrow")
    side = tile_data.shape[1]
    width = user_factor.shape[1]
    touched = item_need.shape[1]
    items_owned = item_slot.shape[0] // wide
    per_user = user_need.shape[1] // wide
    to_all = lambda row: jnp.broadcast_to(row[None], (wide, 1, row.shape[1]))
    need = jnp.concatenate([to_all(user_need), to_all(item_need)], axis=2)
    heard = lax.all_to_all(need, "wide", split_axis=0, concat_axis=0, tiled=True)
    me_wide = lax.axis_index("wide").reshape(1)
    plan = rank(me_wide, tile_live, tile_user, tile_item, touched)
    replies = answer(me_wide, heard, user_slot, user_factor.reshape(-1, side, width), per_user)
    fetched = list(replies)
    for d in reversed(range(1, wide)):
        fetched[d] = lax.ppermute(replies[d], "wide", [(k, k ^ d) for k in range(wide)])
    turned, scale = turn(
        plan,
        tile_word,
        tile_month,
        tile_data,
        word_factor,
        month_factor,
        slots_for(tile_data.shape[0], touched),
    )
    partial = contract(plan, scale, turned, fetched, touched)
    arrived = lax.all_to_all(
        partial.reshape(wide, -1, side, width), "wide", split_axis=0, concat_axis=0, tiled=True
    ).reshape(-1, side, width)
    me = lax.axis_index("narrow").reshape(1)
    pieces = merge(me_wide, me, heard, item_slot, arrived, items_owned, members, touched // wide)
    rows = pieces[0]
    for d in range(1, members):
        got = lax.ppermute(pieces[d], "narrow", [(n, n ^ d) for n in range(members)])
        rows = rows + got.astype(jnp.float32)
    return rows.reshape(-1, width)


def solution(mesh):
    return jax.shard_map(
        body,
        mesh=mesh,
        in_specs=(
            P(("wide", "narrow"), None, None),
            P(("wide", "narrow")),
            P(("wide", "narrow")),
            P(("wide", "narrow")),
            P(("wide", "narrow")),
            P(("wide", "narrow")),
            P(("wide", "narrow"), None),
            P(("wide", "narrow"), None),
            P(),
            P(),
            P("wide", None),
            P(),
            P(),
        ),
        out_specs=P(("wide", "narrow"), None),
        check_vma=False,
    )
```

time: 70.4 us -> 69.7 us (0.990)
  Pallas kernels: 16.9 us -> 14.6 us
  other arithmetic: 0.76 us -> 1.5 us
    pallas_call x3 -> x2, Pallas kernels: 9.96 us -> 6.91 us  [the longest x1 5.03 us: turn(): pl.pallas_call(turn_kernel, out_shape=(jax.ShapeDtypeStruct((slots, side,...]
    concatenate x0 -> x1, other arithmetic: none -> 0.75 us  [body(): need = jnp.concatenate([to_all(user_need), to_all(item_need)], axis=2)]
  transfers between devices with their start and end apart: 12 -> 12, of which waited for: 4 -> 4; matrix products, arithmetic and copies ran while one was open for 0% -> 0% of each run, Pallas kernels for 12% -> 10%
where the time goes in v1:
time: 69.7 us; the launch traced here: 69.2 us
  starting transfers between devices  23.8 us (34%)
  waiting for transfers between devices  20.3 us (29%)
  Pallas kernels  14.6 us (21%)
  local copies, waits for them, and re-layouts  8.26 us (12%)
  other arithmetic  1.5 us (2%)
  between operations  0.76 us (1%)
    ppermute x7, starting transfers between devices, body(): lax.ppermute(replies[d], 'wide', [(k, k ^ d) for k in range(wide)])  11.2 us
    all_to_all x1, waiting for transfers between devices, body(): lax.all_to_all(partial.reshape(wide, -1, side, width), 'wide', split_axis...  8.15 us
    unnamed x18, local copies, waits for them, and re-layouts  7.67 us
    all_to_all x1, starting transfers between devices, body(): lax.all_to_all(need, 'wide', split_axis=0, concat_axis=0, tiled=True)  7.28 us
    ppermute x3, waiting for transfers between devices, body(): lax.ppermute(pieces[d], 'narrow', [(n, n ^ d) for n in range(members)])  6.32 us
    pallas_call x1, Pallas kernels, contract(): pl.pallas_call(contract_kernel, out_shape=jax.ShapeDtypeStruct((touched,...  6.14 us
    all_to_all x1, waiting for transfers between devices, body(): lax.all_to_all(need, 'wide', split_axis=0, concat_axis=0, tiled=True)  5.77 us
    pallas_call x1, Pallas kernels, turn(): pl.pallas_call(turn_kernel, out_shape=(jax.ShapeDtypeStruct((slots, side,...  5.03 us
  transfers between devices with their start and end apart: 12, of which 4 were waited for; matrix products, arithmetic and copies ran while one was open for 0% of the time, Pallas kernels for 10%

profile of v1, /device:TPU:0, one launch (start us, length us, event | category | flops | bytes accessed | tf_op | source)
XLA Modules:
  0.0 69.2 jit_solution(11709283221110048644)
XLA Ops:
  0.0 0.7 %pad_add_fusion = s32[24]{0:T(128)S(1)} fusion(s32[8]{0:T(128)} %bitcast.12, s32[16]{0:T(128)} %bitcast.13), kind=kLoop, calls=%fused_computation.1 | loop fusion | flops 24 | bytes 192 | tf_op jit(solution)/shard_map/concatenate | solution.py:276
  0.7 0.6 broadcast.4
  1.3 7.3 %all-to-all-start = ((s32[8,1,24]{2,1,0:T(1,128)}), s32[8,1,24]{2,1,0:T(1,128)S(1)}, u32[]{:S(2)}, u32[]{:S(2)}) async-start(s32[8,1,24]{2,1,0:T(1,128)} %broadcast.4), calls=%async_computation | async-start | bytes 8192 | tf_op jit(solution)/shard_map/all_to_all | solution.py:277
  9.3 5.8 %all-to-all-done.heard = s32[8,1,24]{2,1,0:T(1,128)S(1)} async-done(((s32[8,1,24]{2,1,0:T(1,128)}), s32[8,1,24]{2,1,0:T(1,128)S(1)}, u32[]{:S(2)}, u32[]{:S(2)}) %all-to-all-start) | async-done | bytes 800 | tf_op jit(solution)/shard_map/all_to_all | solution.py:277
  15.0 0.0 copy-start.7
  15.0 1.0 %copy-done.7 = bf16[2048,128]{1,0:T(8,128)(2,1)S(1)} copy-done((bf16[2048,128]{1,0:T(8,128)(2,1)S(1)}, bf16[2048,128]{1,0:T(8,128)(2,1)}, u32[]{:S(2)}) %copy-start.7) | copy-done | bytes 524312
  16.1 0.0 copy-start.8
  16.1 0.7 copy-done.8
  16.7 0.7 answer.1
  17.4 0.6 collective-permute-start
  18.0 0.0 copy-start.2
  18.0 0.0 copy-start.4
  18.0 0.6 collective-permute-start.1
  18.6 1.9 %rank.1.plan = s32[16,512]{1,0:T(8,128)} custom-call(s32[1]{0:T(128)} %bitcast.me.owner, s32[1]{0:T(128)S(6)} %copy.15.live, s32[320]{0:T(512)} %user.1, s32[320]{0:T(512)} %item.1), custom_call_target="tpu_custom_call" | custom-call | flops 8589934592 | bytes 33554432 | tf_op jit(solution)/shard_map/rank/pallas_call | solution.py:72
  20.5 0.0 copy-start.6
  20.5 2.4 %collective-permute-start.2 = (bf16[2,128,128]{2,1,0:T(8,128)(2,1)S(1)}, bf16[2,128,128]{2,1,0:T(8,128)(2,1)S(1)}, u32[]{:S(2)}, u32[]{:S(2)}) collective-permute-start(bf16[2,128,128]{2,1,0:T(8,128)(2,1)S(1)} %get-tuple-element.24), channel_id=1, source_target_pairs={{0,12},{4,8},{8,4},{12,0},{16,28},{20,24},{24,20},{28,16},{1,13},{... | collective-permute-start | bytes 196616 | tf_op jit(solution)/shard_map/ppermute | solution.py:283
  22.9 0.6 collective-permute-start.3
  23.4 2.4 %collective-permute-start.4 = (bf16[2,128,128]{2,1,0:T(8,128)(2,1)S(1)}, bf16[2,128,128]{2,1,0:T(8,128)(2,1)S(1)}, u32[]{:S(2)}, u32[]{:S(2)}) collective-permute-start(bf16[2,128,128]{2,1,0:T(8,128)(2,1)S(1)} %get-tuple-element.26), channel_id=1, source_target_pairs={{0,20},{4,16},{8,28},{12,24},{16,4},{20,0},{24,12},{28,8},{1,21},{... | collective-permute-start | bytes 196616 | tf_op jit(solution)/shard_map/ppermute | solution.py:283
  25.8 0.0 collective-permute-done.refs_1_
  25.8 0.6 collective-permute-start.5
  26.4 0.0 collective-permute-done.1.refs_2_
  26.4 4.1 %collective-permute-start.6 = (bf16[2,128,128]{2,1,0:T(8,128)(2,1)S(1)}, bf16[2,128,128]{2,1,0:T(8,128)(2,1)S(1)}, u32[]{:S(2)}, u32[]{:S(2)}) collective-permute-start(bf16[2,128,128]{2,1,0:T(8,128)(2,1)S(1)} %get-tuple-element.28), channel_id=1, source_target_pairs={{0,28},{4,24},{8,20},{12,16},{16,12},{20,8},{24,4},{28,0},{1,29},{... | collective-permute-start | bytes 196616 | tf_op jit(solution)/shard_map/ppermute | solution.py:283
  30.5 0.0 copy-done.2
  30.5 0.0 copy-done.4
  30.5 0.0 copy-done.5
  30.5 0.0 copy-start
  30.5 4.0 %copy-done = bf16[320,128,128]{2,1,0:T(8,128)(2,1)S(1)} copy-done((bf16[320,128,128]{2,1,0:T(8,128)(2,1)S(1)}, bf16[320,128,128]{2,1,0:T(8,128)(2,1)}, u32[]{:S(2)}) %copy-start) | copy-done | bytes 10485784
  34.5 1.2 %copy-done.1 = bf16[4096,128]{1,0:T(8,128)(2,1)S(1)} copy-done((bf16[4096,128]{1,0:T(8,128)(2,1)S(1)}, bf16[4096,128]{1,0:T(8,128)(2,1)}, u32[]{:S(2)}) %copy-start.1) | copy-done | bytes 1048600
  35.7 0.0 copy-start.3
  35.7 0.8 %copy-done.3 = s32[16,512]{1,0:T(8,128)S(1)} copy-done((s32[16,512]{1,0:T(8,128)S(1)}, s32[16,512]{1,0:T(8,128)}, u32[]{:S(2)}) %copy-start.3) | copy-done | bytes 32792
  36.5 5.0 %turn.1 = (bf16[448,128,128]{2,1,0:T(8,128)(2,1)S(1)}, f32[448,128]{1,0:T(8,128)S(1)}) custom-call(s32[16,512]{1,0:T(8,128)S(1)} %copy-done.3, s32[320]{0:T(512)S(1)} %copy-done.4, s32[320]{0:T(512)S(1)} %copy-done.5, bf16[320,128,128]{2,1,0:T(8,128)(2,1)S(1)} %copy-done, bf16[4096,128]{1,0:T(8,128)(2,1)S(1)} %copy-done.1, bf16[1000,128]{1,0:T(8,128)(2,1)S(1)} %copy-done.2), custom_call_target="tpu_custom_call" | custom-call | flops 1073741824 | bytes 20971520 | tf_op jit(solution)/shard_map/turn/pallas_call | solution.py:123
  41.5 0.0 collective-permute-done.2.refs_3_
  41.5 0.0 collective-permute-done.3.refs_4_
  41.5 0.0 collective-permute-done.4.refs_5_
  41.6 0.0 collective-permute-done.5.refs_6_
  41.6 0.0 collective-permute-done.6.refs_7_
  41.6 6.1 %contract.1 = bf16[8,128,128]{2,1,0:T(8,128)(2,1)} custom-call(s32[16,512]{1,0:T(8,128)S(1)} %copy-done.3, f32[448,128]{1,0:T(8,128)S(1)} %get-tuple-element.19.scale, bf16[448,128,128]{2,1,0:T(8,128)(2,1)S(1)} %get-tuple-element.20.turned, bf16[2,128,128]{2,1,0:T(8,128)(2,1)S(1)} %get-tuple-element.21.refs_0_, ...), custom_call_target="tpu_custom_call" | custom-call | flops 1879048192 | bytes 7340032 | tf_op jit(solution)/shard_map/contract/pallas_call | solution.py:198
  47.7 3.4 %all-to-all-start.1 = ((bf16[8,1,128,128]{3,2,1,0:T(8,128)(2,1)}), bf16[8,1,128,128]{3,2,1,0:T(8,128)(2,1)S(1)}, u32[]{:S(2)}, u32[]{:S(2)}) async-start(bf16[8,1,128,128]{3,2,1,0:T(8,128)(2,1)} %bitcast.6), calls=%async_computation.1 | async-start | bytes 524288 | tf_op jit(solution)/shard_map/all_to_all | solution.py:294
  51.1 8.2 %all-to-all-done.1 = bf16[8,1,128,128]{3,2,1,0:T(8,128)(2,1)S(1)} async-done(((bf16[8,1,128,128]{3,2,1,0:T(8,128)(2,1)}), bf16[8,1,128,128]{3,2,1,0:T(8,128)(2,1)S(1)}, u32[]{:S(2)}, u32[]{:S(2)}) %all-to-all-start.1) | async-done | bytes 262176 | tf_op jit(solution)/shard_map/all_to_all | solution.py:294
  59.3 0.0 copy-done.6
  59.3 0.9 %merge.1 = (f32[4,128,128]{2,1,0:T(8,128)S(1)}, bf16[4,128,128]{2,1,0:T(8,128)(2,1)S(1)}, bf16[4,128,128]{2,1,0:T(8,128)(2,1)S(1)}, bf16[4,128,128]{2,1,0:T(8,128)(2,1)S(1)}) custom-call(s32[1]{0:T(128)} %bitcast.me.owner, s32[1]{0:T(128)} %bitcast.1.me, s32[8,1,24]{2,1,0:T(1,128)S(1)} %all-to-all-done.heard, s32[128]{0:T(128)S(1)} %copy-done.6, ...), custom_call_target="tpu_custom_call" | custom-call | tf_op jit(solution)/shard_map/merge/pallas_call | solution.py:242
  60.2 0.1 collective-permute-start.7
  60.3 0.4 collective-permute-start.8
  60.6 1.5 %collective-permute-start.9 = (bf16[4,128,128]{2,1,0:T(8,128)(2,1)S(1)}, bf16[4,128,128]{2,1,0:T(8,128)(2,1)S(1)}, u32[]{:S(2)}, u32[]{:S(2)}) collective-permute-start(bf16[4,128,128]{2,1,0:T(8,128)(2,1)S(1)} %get-tuple-element.32), channel_id=1, source_target_pairs={{0,3},{1,2},{2,1},{3,0},{4,7},{5,6},{6,5},{7,4},{8,11},{9,10},{10,... | collective-permute-start | bytes 393224 | tf_op jit(solution)/shard_map/ppermute | solution.py:301
  62.1 0.0 collective-permute-done.7
  62.1 4.6 %collective-permute-done.8 = bf16[4,128,128]{2,1,0:T(8,128)(2,1)S(1)} collective-permute-done((bf16[4,128,128]{2,1,0:T(8,128)(2,1)S(1)}, bf16[4,128,128]{2,1,0:T(8,128)(2,1)S(1)}, u32[]{:S(2)}, u32[]{:S(2)}) %collective-permute-start.8) | collective-permute-done | bytes 131104 | tf_op jit(solution)/shard_map/ppermute | solution.py:301
  66.7 1.7 %collective-permute-done.9 = bf16[4,128,128]{2,1,0:T(8,128)(2,1)S(1)} collective-permute-done((bf16[4,128,128]{2,1,0:T(8,128)(2,1)S(1)}, bf16[4,128,128]{2,1,0:T(8,128)(2,1)S(1)}, u32[]{:S(2)}, u32[]{:S(2)}) %collective-permute-start.9) | collective-permute-done | bytes 131104 | tf_op jit(solution)/shard_map/ppermute | solution.py:301
  68.4 0.8 %convert_add_fusion = f32[4,128,128]{2,1,0:T(8,128)} fusion(bf16[4,128,128]{2,1,0:T(8,128)(2,1)S(1)} %collective-permute-done.9, bf16[4,128,128]{2,1,0:T(8,128)(2,1)S(1)} %collective-permute-done.8, f32[4,128,128]{2,1,0:T(8,128)S(1)} %get-tuple-element.29, bf16[4,128,128]{2,1,0:T(8,128)(2,1)S(1)} %collective-permute-done.7), kind=kLoop, calls=%fused_computation | loop fusion | flops 393216 | bytes 917504 | tf_op jit(solution)/shard_map/add | solution.py:302
  (2 shorter events, 0.0 us)
Async XLA Ops:
  1.3 13.7 %all-to-all-start = ((s32[8,1,24]{2,1,0:T(1,128)}), s32[8,1,24]{2,1,0:T(1,128)S(1)}, u32[]{:S(2)}, u32[]{:S(2)}) async-start(s32[8,1,24]{2,1,0:T(1,128)} %broadcast.4), calls=%async_computation | async-start | bytes 8192 | tf_op jit(solution)/shard_map/all_to_all | solution.py:277
  15.0 1.0 %copy-start.7 = (bf16[2048,128]{1,0:T(8,128)(2,1)S(1)}, bf16[2048,128]{1,0:T(8,128)(2,1)}, u32[]{:S(2)}) copy-start(bf16[2048,128]{1,0:T(8,128)(2,1)} %param.23) | copy-start | bytes 1572868
  16.1 0.7 copy-start.8
  17.4 8.4 %collective-permute-start = (bf16[2,128,128]{2,1,0:T(8,128)(2,1)S(1)}, bf16[2,128,128]{2,1,0:T(8,128)(2,1)S(1)}, u32[]{:S(2)}, u32[]{:S(2)}) collective-permute-start(bf16[2,128,128]{2,1,0:T(8,128)(2,1)S(1)} %get-tuple-element.22), channel_id=1, source_target_pairs={{0,4},{4,0},{8,12},{12,8},{16,20},{20,16},{24,28},{28,24},{1,5},{5... | collective-permute-start | bytes 196616 | tf_op jit(solution)/shard_map/ppermute | solution.py:283
  18.0 12.5 %copy-start.2 = (bf16[1000,128]{1,0:T(8,128)(2,1)S(1)}, bf16[1000,128]{1,0:T(8,128)(2,1)}, u32[]{:S(2)}) copy-start(bf16[1000,128]{1,0:T(8,128)(2,1)} %months.1) | copy-start | bytes 768004
  18.0 12.5 %copy-start.4 = (s32[320]{0:T(512)S(1)}, s32[320]{0:T(512)}, u32[]{:S(2)}) copy-start(s32[320]{0:T(512)} %word.1) | copy-start | bytes 3844
  18.0 12.5 %copy-start.5 = (s32[320]{0:T(512)S(1)}, s32[320]{0:T(512)}, u32[]{:S(2)}) copy-start(s32[320]{0:T(512)} %month.1) | copy-start | bytes 3844
  18.0 8.3 %collective-permute-start.1 = (bf16[2,128,128]{2,1,0:T(8,128)(2,1)S(1)}, bf16[2,128,128]{2,1,0:T(8,128)(2,1)S(1)}, u32[]{:S(2)}, u32[]{:S(2)}) collective-permute-start(bf16[2,128,128]{2,1,0:T(8,128)(2,1)S(1)} %get-tuple-element.23), channel_id=1, source_target_pairs={{0,8},{4,12},{8,0},{12,4},{16,24},{20,28},{24,16},{28,20},{1,9},{5... | collective-permute-start | bytes 196616 | tf_op jit(solution)/shard_map/ppermute | solution.py:283
  20.5 38.8 %copy-start.6 = (s32[128]{0:T(128)S(1)}, s32[128]{0:T(128)}, u32[]{:S(2)}) copy-start(s32[128]{0:T(128)} %slot.3) | copy-start | bytes 1540
  20.5 21.0 %collective-permute-start.2 = (bf16[2,128,128]{2,1,0:T(8,128)(2,1)S(1)}, bf16[2,128,128]{2,1,0:T(8,128)(2,1)S(1)}, u32[]{:S(2)}, u32[]{:S(2)}) collective-permute-start(bf16[2,128,128]{2,1,0:T(8,128)(2,1)S(1)} %get-tuple-element.24), channel_id=1, source_target_pairs={{0,12},{4,8},{8,4},{12,0},{16,28},{20,24},{24,20},{28,16},{1,13},{... | collective-permute-start | bytes 196616 | tf_op jit(solution)/shard_map/ppermute | solution.py:283
  22.9 18.7 %collective-permute-start.3 = (bf16[2,128,128]{2,1,0:T(8,128)(2,1)S(1)}, bf16[2,128,128]{2,1,0:T(8,128)(2,1)S(1)}, u32[]{:S(2)}, u32[]{:S(2)}) collective-permute-start(bf16[2,128,128]{2,1,0:T(8,128)(2,1)S(1)} %get-tuple-element.25), channel_id=1, source_target_pairs={{0,16},{4,20},{8,24},{12,28},{16,0},{20,4},{24,8},{28,12},{1,17},{... | collective-permute-start | bytes 196616 | tf_op jit(solution)/shard_map/ppermute | solution.py:283
  23.4 18.1 %collective-permute-start.4 = (bf16[2,128,128]{2,1,0:T(8,128)(2,1)S(1)}, bf16[2,128,128]{2,1,0:T(8,128)(2,1)S(1)}, u32[]{:S(2)}, u32[]{:S(2)}) collective-permute-start(bf16[2,128,128]{2,1,0:T(8,128)(2,1)S(1)} %get-tuple-element.26), channel_id=1, source_target_pairs={{0,20},{4,16},{8,28},{12,24},{16,4},{20,0},{24,12},{28,8},{1,21},{... | collective-permute-start | bytes 196616 | tf_op jit(solution)/shard_map/ppermute | solution.py:283
  25.8 15.8 %collective-permute-start.5 = (bf16[2,128,128]{2,1,0:T(8,128)(2,1)S(1)}, bf16[2,128,128]{2,1,0:T(8,128)(2,1)S(1)}, u32[]{:S(2)}, u32[]{:S(2)}) collective-permute-start(bf16[2,128,128]{2,1,0:T(8,128)(2,1)S(1)} %get-tuple-element.27), channel_id=1, source_target_pairs={{0,24},{4,28},{8,16},{12,20},{16,8},{20,12},{24,0},{28,4},{1,25},{... | collective-permute-start | bytes 196616 | tf_op jit(solution)/shard_map/ppermute | solution.py:283
  26.4 15.2 %collective-permute-start.6 = (bf16[2,128,128]{2,1,0:T(8,128)(2,1)S(1)}, bf16[2,128,128]{2,1,0:T(8,128)(2,1)S(1)}, u32[]{:S(2)}, u32[]{:S(2)}) collective-permute-start(bf16[2,128,128]{2,1,0:T(8,128)(2,1)S(1)} %get-tuple-element.28), channel_id=1, source_target_pairs={{0,28},{4,24},{8,20},{12,16},{16,12},{20,8},{24,4},{28,0},{1,29},{... | collective-permute-start | bytes 196616 | tf_op jit(solution)/shard_map/ppermute | solution.py:283
  30.5 4.0 %copy-start = (bf16[320,128,128]{2,1,0:T(8,128)(2,1)S(1)}, bf16[320,128,128]{2,1,0:T(8,128)(2,1)}, u32[]{:S(2)}) copy-start(bf16[320,128,128]{2,1,0:T(8,128)(2,1)} %tiles.1) | copy-start | bytes 31457284
  34.5 1.2 %copy-start.1 = (bf16[4096,128]{1,0:T(8,128)(2,1)S(1)}, bf16[4096,128]{1,0:T(8,128)(2,1)}, u32[]{:S(2)}) copy-start(bf16[4096,128]{1,0:T(8,128)(2,1)} %words.1) | copy-start | bytes 3145732
  35.7 0.8 %copy-start.3 = (s32[16,512]{1,0:T(8,128)S(1)}, s32[16,512]{1,0:T(8,128)}, u32[]{:S(2)}) copy-start(s32[16,512]{1,0:T(8,128)} %rank.1.plan) | copy-start | bytes 98308
  47.7 11.6 %all-to-all-start.1 = ((bf16[8,1,128,128]{3,2,1,0:T(8,128)(2,1)}), bf16[8,1,128,128]{3,2,1,0:T(8,128)(2,1)S(1)}, u32[]{:S(2)}, u32[]{:S(2)}) async-start(bf16[8,1,128,128]{3,2,1,0:T(8,128)(2,1)} %bitcast.6), calls=%async_computation.1 | async-start | bytes 524288 | tf_op jit(solution)/shard_map/all_to_all | solution.py:294
  60.2 1.9 %collective-permute-start.7 = (bf16[4,128,128]{2,1,0:T(8,128)(2,1)S(1)}, bf16[4,128,128]{2,1,0:T(8,128)(2,1)S(1)}, u32[]{:S(2)}, u32[]{:S(2)}) collective-permute-start(bf16[4,128,128]{2,1,0:T(8,128)(2,1)S(1)} %get-tuple-element.30), channel_id=1, source_target_pairs={{0,1},{1,0},{2,3},{3,2},{4,5},{5,4},{6,7},{7,6},{8,9},{9,8},{10,11... | collective-permute-start | bytes 393224 | tf_op jit(solution)/shard_map/ppermute | solution.py:301
  60.3 6.4 %collective-permute-start.8 = (bf16[4,128,128]{2,1,0:T(8,128)(2,1)S(1)}, bf16[4,128,128]{2,1,0:T(8,128)(2,1)S(1)}, u32[]{:S(2)}, u32[]{:S(2)}) collective-permute-start(bf16[4,128,128]{2,1,0:T(8,128)(2,1)S(1)} %get-tuple-element.31), channel_id=1, source_target_pairs={{0,2},{1,3},{2,0},{3,1},{4,6},{5,7},{6,4},{7,5},{8,10},{9,11},{10,... | collective-permute-start | bytes 393224 | tf_op jit(solution)/shard_map/ppermute | solution.py:301
  60.6 7.8 %collective-permute-start.9 = (bf16[4,128,128]{2,1,0:T(8,128)(2,1)S(1)}, bf16[4,128,128]{2,1,0:T(8,128)(2,1)S(1)}, u32[]{:S(2)}, u32[]{:S(2)}) collective-permute-start(bf16[4,128,128]{2,1,0:T(8,128)(2,1)S(1)} %get-tuple-element.32), channel_id=1, source_target_pairs={{0,3},{1,2},{2,1},{3,0},{4,7},{5,6},{6,5},{7,4},{8,11},{9,10},{10,... | collective-permute-start | bytes 393224 | tf_op jit(solution)/shard_map/ppermute | solution.py:301
